TPU v7x, 32 devices: a whole 2x2x4 slice. The times are simulated.
32 devices in a mesh: group: 2 (over x), src: 16 (over z, y, core).
Axes of the slice: x: 2, y: 2, z: 4, core: 2. Of those that a mesh axis runs over, the one named last changes fastest.
Arguments:
- rcv_points: float32 [3, 4096], P(None, ('group', 'src')), parts along dimension 1, may hold values from -1 to 1
- rcv_normals: float32 [3, 4096], P(None, ('group', 'src')), parts along dimension 1, may hold values from -4 to 4
- left_modes: float32 [8, 4096], P(None, ('group', 'src')), parts along dimension 1, may hold values from -5 to 5
- vertices: float32 [3, 2048], P(None, ('group', 'src')), parts along dimension 1, may hold values from -1 to 1
- connect: int32 [2, 4096], P(None, ('group', 'src')), parts along dimension 1, may hold values from 0 to 1023, as said below
- right_modes: float32 [8, 4096], P(None, ('group', 'src')), parts along dimension 1, may hold values from -0.125 to 0.125
- mode_weights: float32 [16], P('group'), parts along dimension 0, may hold values from 0.25 to 1
Outputs:
- rcv_grad: float32 [6, 4096], P(None, ('group', 'src')), parts along dimension 1
- vert_grad: float32 [3, 2048], P(None, ('group', 'src')), parts along dimension 1
There are 2 independent parts, one for each index of `group`. A program takes and returns all parts, laid end to end along the dimension named above; each array names one. Nothing has to cross between parts.
Inputs may be any that keep to these rules, and one draw needn't show every extreme that they name: `connect`: a panel's first vertex is one of the 64 vertices held at the same index of src as the panel, and its second vertex is the next vertex number.
All inputs are finite; a program needn't handle non-finite values.
Results may differ from a plain program's by a relative error of at most 0.0003.
Values sent between devices are 32-bit elements; how exact they have to be, the bound alone decides.
No kernel may reach another device: no remote copies, remote signals or barrier semaphores. Data moves between devices by JAX's collectives and lax.ppermute only.
A program may use at most 64 MiB of HBM per device.

v0:
```python
import math
import jax
import jax.numpy as jnp
from jax import lax
from jax.sharding import PartitionSpec as P

core_term = 0.05
inverse_four_pi = 0.25 / math.pi


def shifted(value, axis, steps):
    count = lax.axis_size(axis)
    leading, last = (max(0, -steps), min(count, count - steps))
    return lax.ppermute(value, axis, [(source, source + steps) for source in range(leading, last)])


def lift_points(raw):
    return jnp.stack([raw[0], raw[1], 0.5 + 0.2 * raw[2]])


def place_points(raw):
    return jnp.stack([raw[0], raw[1], 0.2 * raw[2]])


def tile_energy(points, normals, first_end, second_end, coefficient):
    rel_first = points[:, None, :] - first_end[:, :, None]
    rel_second = points[:, None, :] - second_end[:, :, None]
    segment = (second_end - first_end)[:, :, None]
    cross_x = rel_first[1] * rel_second[2] - rel_first[2] * rel_second[1]
    cross_y = rel_first[2] * rel_second[0] - rel_first[0] * rel_second[2]
    cross_z = rel_first[0] * rel_second[1] - rel_first[1] * rel_second[0]
    cross_sq = cross_x * cross_x + cross_y * cross_y + cross_z * cross_z
    dist_first = jnp.sqrt(jnp.sum(rel_first * rel_first, axis=0))
    dist_second = jnp.sqrt(jnp.sum(rel_second * rel_second, axis=0))
    along_term = jnp.sum(segment * (rel_first / dist_first - rel_second / dist_second), axis=0)
    span_sq = jnp.sum(segment * segment, axis=0)
    denominator = cross_sq + core_term * (span_sq + 1.0)
    normal_term = (
        normals[0][None, :] * cross_x
        + normals[1][None, :] * cross_y
        + normals[2][None, :] * cross_z
    )
    influence = inverse_four_pi * normal_term * along_term / denominator
    return jnp.sum(coefficient * influence)


def tile_gradients(points, normals, first_end, second_end, coefficient):
    return jax.grad(tile_energy, argnums=(0, 1, 2, 3))(
        points, normals, first_end, second_end, coefficient
    )


def on_device(rcv_points, rcv_normals, left_modes, vertices, connect, right_modes, mode_weights):
    own_count = vertices.shape[1]
    next_first = shifted(vertices[:, :1], "src", -1)
    extended = jnp.concatenate([vertices, next_first], axis=1)
    places = place_points(extended)
    base_vertex = lax.axis_index("src") * own_count
    local_first = connect[0] - base_vertex
    local_second = local_first + 1
    first_end = places[:, local_first]
    second_end = places[:, local_second]
    points = lift_points(rcv_points)
    chain_scale = jnp.array([1.0, 1.0, 0.2], dtype=jnp.float32)[:, None]
    weighted = right_modes * mode_weights[:, None]
    receiver_count = rcv_points.shape[1] * lax.axis_size("src")
    source_count = connect.shape[1]
    start_totals = (
        jnp.zeros((3, source_count), jnp.float32),
        jnp.zeros((3, source_count), jnp.float32),
        jnp.zeros((6, receiver_count), jnp.float32),
    )
    shard_points = lax.all_gather(points, "src", axis=1, tiled=True)
    shard_normals = lax.all_gather(rcv_normals, "src", axis=1, tiled=True)
    shard_left = lax.all_gather(left_modes, "src", axis=1, tiled=True)
    row_count = shard_points.shape[1]
    width_rows = math.gcd(row_count, 2048)

    def advance(number, inner):
        sum_first, sum_second, receiver_buffer = inner
        local_start = number * width_rows
        block_points = lax.dynamic_slice_in_dim(shard_points, local_start, width_rows, 1)
        block_normals = lax.dynamic_slice_in_dim(shard_normals, local_start, width_rows, 1)
        block_left = lax.dynamic_slice_in_dim(shard_left, local_start, width_rows, 1)
        coefficient = jnp.einsum("mj,mi->ji", weighted, block_left, precision=lax.Precision.HIGHEST)
        grads = tile_gradients(block_points, block_normals, first_end, second_end, coefficient)
        rows_out = jnp.concatenate([grads[0] * chain_scale, grads[1]], axis=0)
        receiver_buffer = lax.dynamic_update_slice_in_dim(receiver_buffer, rows_out, local_start, 1)
        return (sum_first + grads[2], sum_second + grads[3], receiver_buffer)

    sum_first, sum_second, receiver_buffer = lax.fori_loop(
        0, row_count // width_rows, advance, start_totals
    )
    rcv_grad = lax.psum_scatter(receiver_buffer, "src", scatter_dimension=1, tiled=True)
    vertex_partial = jnp.zeros((3, own_count + 1), jnp.float32)
    vertex_partial = (
        vertex_partial.at[:, local_first].add(sum_first).at[:, local_second].add(sum_second)
    )
    incoming = shifted(vertex_partial[:, own_count:], "src", 1)
    own_part = vertex_partial[:, :own_count]
    own_part = jnp.concatenate([own_part[:, :1] + incoming, own_part[:, 1:]], axis=1)
    vert_grad = own_part * chain_scale
    return (rcv_grad, vert_grad)


def solution(mesh):
    in_specs = (
        P(None, ("group", "src")),
        P(None, ("group", "src")),
        P(None, ("group", "src")),
        P(None, ("group", "src")),
        P(None, ("group", "src")),
        P(None, ("group", "src")),
        P("group"),
    )
    out_specs = (P(None, ("group", "src")), P(None, ("group", "src")))
    return jax.shard_map(
        on_device, mesh=mesh, in_specs=in_specs, out_specs=out_specs, check_vma=False
    )
```

profile of v0, /device:TPU:0, one launch (start us, length us, event | category | flops | bytes accessed | tf_op | source)
XLA Modules:
  0.0 154.4 jit_solution(849035136935577808)
XLA Ops:
  7.2 1.3 collective-permute-start
  8.5 0.7 multiply_add_fusion.1
  9.2 0.7 slice.81
  9.9 23.8 %all_gather.10 = f32[3,2048]{1,0:T(4,128)S(1)} all-gather(f32[3,128]{1,0:T(4,128)S(1)} %pad_maximum_fusion.3), channel_id=1, replica_groups=mesh['group'=2,'src'=16] {'src'}, dimensions={1}, use_global_device_ids=true | all-gather | bytes 26112 | tf_op jit(solution)/shard_map/all_gather | solution.py:73
  33.7 17.7 %all_gather.9 = f32[3,2048]{1,0:T(4,128)S(1)} all-gather(f32[3,128]{1,0:T(4,128)} %param.9), channel_id=1, replica_groups=mesh['group'=2,'src'=16] {'src'}, dimensions={1}, use_global_device_ids=true | all-gather | bytes 26112 | tf_op jit(solution)/shard_map/all_gather | solution.py:74
  51.4 19.2 %all_gather.11 = f32[8,2048]{1,0:T(8,128)S(1)} all-gather(f32[8,128]{1,0:T(8,128)} %param.10), channel_id=1, replica_groups=mesh['group'=2,'src'=16] {'src'}, dimensions={1}, use_global_device_ids=true | all-gather | bytes 69632 | tf_op jit(solution)/shard_map/all_gather | solution.py:75
  70.6 0.7 fusion.24
  71.3 0.8 pad_maximum_fusion.1
  72.1 0.1 copy.26
  72.2 0.6 gather_fusion.1
  72.9 0.7 gather_fusion
  73.7 0.8 fusion.15
  74.6 0.3 multiply_divide_fusion.1
  74.9 0.3 multiply_divide_fusion.2
  75.3 1.8 %divide_multiply_fusion.1 = (f32[128,2048]{1,0:T(8,128)S(1)}, f32[128,2048]{1,0:T(8,128)S(1)}, f32[128,2048]{1,0:T(8,128)S(1)}, f32[128,2048]{1,0:T(8,128)S(1)},...) fusion(f32[128]{0:T(128)S(1)} %add_multiply_fusion.2, f32[2048]{0:T(1024)S(1)} %bitcast.136, ...), kind=kOutput, calls=%fused_computation.109 | convolution fusion | flops 31196160 | bytes 13726240 | tf_op jit(solution)/shard_map/while/body/eval_jaxpr/mj,mi->ji/dot_general | solution.py:85
  77.1 2.5 %multiply_reduce_fusion = (f32[3,128]{1,0:T(4,128)S(1)}, f32[128,2048]{1,0:T(8,128)S(1)}, f32[128,2048]{1,0:T(8,128)S(1)}, f32[128,2048]{1,0:T(8,128)S(1)}) fusion(f32[128,2048]{1,0:T(8,128)S(1)} %get-tuple-element.62, f32[128,2048]{1,0:T(8,128)S(1)} %get-tuple-element.92, f32[3,128]{1,0:T(4,128)S(1)} %bitcast.127, f32[128,2048]{1,0:T(8,128)S(1)} %get-tuple-element.94, ...), kind=kLoop, calls=%fused_computation.36 | loop fusion | flops 12582528 | bytes 8419328 | tf_op jit(solution)/shard_map/while/body/eval_jaxpr/transpose(jvp())/reduce_sum | solution.py:35
  79.6 0.2 multiply_multiply_fusion.3
  79.8 0.2 multiply_multiply_fusion.1
  80.1 0.6 fusion.28
  80.6 2.0 %multiply_bitcast_fusion.5 = (f32[1,128,2048]{2,1,0:T(8,128)}, f32[128,2048]{1,0:T(8,128)}, f32[128,2048]{1,0:T(8,128)S(1)}) fusion(f32[3,128,2048]{2,1,0:T(8,128)S(1)} %get-tuple-element.95, f32[128,2048]{1,0:T(8,128)S(1)} %get-tuple-element.67, f32[128,2048]{1,0:T(8,128)S(1)} %get-tuple-element.54, f32[2048]{0:T(1024)S(1)} %broadcast_multiply_fusion.2, ...), kind=kLoop, calls=%fused_computation.57 | loop fusion | flops 2359296 | bytes 9445376 | tf_op jit(solution)/shard_map/while/body/eval_jaxpr/transpose(jvp())/broadcast_in_dim | solution.py:31
  82.6 2.2 %multiply_bitcast_fusion.3 = (f32[1,128,2048]{2,1,0:T(8,128)S(1)}, f32[128,2048]{1,0:T(8,128)}, f32[1,128,2048]{2,1,0:T(8,128)S(1)}, f32[128,2048]{1,0:T(8,128)}...) fusion(f32[3,128,2048]{2,1,0:T(8,128)S(1)} %get-tuple-element.95, f32[128,2048]{1,0:T(8,128)S(1)} %get-tuple-element.66, ...), kind=kLoop, calls=%fused_computation.55 | loop fusion | flops 5236736 | bytes 11575296 | tf_op jit(solution)/shard_map/while/body/eval_jaxpr/transpose(jvp())/broadcast_in_dim | solution.py:30
  84.9 4.8 %multiply_bitcast_fusion.11 = (f32[1,128,2048]{2,1,0:T(8,128)S(1)}, f32[1,128,2048]{2,1,0:T(8,128)S(1)}, f32[1,128,2048]{2,1,0:T(8,128)S(1)}, f32[1,128,2048]{2,...) fusion(f32[128,2048]{1,0:T(8,128)} %get-tuple-element.56, ...), kind=kLoop, calls=%fused_computation.65 | loop fusion | flops 3145728 | bytes 18874368 | tf_op jit(solution)/shard_map/while/body/eval_jaxpr/transpose(jvp())/broadcast_in_dim | solution.py:31
  89.7 3.4 %fusion.27 = (f32[3,128]{1,0:T(4,128)S(1)}, f32[3,2048]{1,0:T(4,128)S(1)}) fusion(f32[1,128,2048]{2,1,0:T(8,128)} %get-tuple-element.88, f32[1,128,2048]{2,1,0:T(8,128)S(1)} %get-tuple-element.70, f32[1,128,2048]{2,1,0:T(8,128)} %get-tuple-element.89, f32[1,128,2048]{2,1,0:T(8,128)S(1)} %get-tuple-element.58, f32[1,128,2048]{2,1,0:T(8,128)} %get-tuple-element.90, ...), kind=kLoop, calls=%fused_computation.111 | loop fusion | flops 11003520 | bytes 9490944 | tf_op jit(solution)/shard_map/while/body/eval_jaxpr/transpose(jvp())/reduce_sum | solution.py:26
  93.1 1.9 %fusion.26 = (f32[3,128]{1,0:T(4,128)S(1)}, f32[3,2048]{1,0:T(4,128)S(1)}) fusion(f32[1,128,2048]{2,1,0:T(8,128)S(1)} %get-tuple-element.84, f32[1,128,2048]{2,1,0:T(8,128)S(1)} %get-tuple-element.85, f32[1,128,2048]{2,1,0:T(8,128)S(1)} %get-tuple-element.86, f32[1,128,2048]{2,1,0:T(8,128)S(1)} %copy-done, f32[1,128,2048]{2,1,0:T(8,128)S(1)} %get-tuple-element.73, ...), kind=kLoop, calls=%fused_computation.110 | loop fusion | flops 11789952 | bytes 9490944 | tf_op jit(solution)/shard_map/while/body/eval_jaxpr/transpose(jvp())/reduce_sum | solution.py:27
  95.0 0.1 copy.31
  95.2 1.0 scatter_custom_fusion
  96.2 1.2 scatter_fusion
  97.6 0.6 pad_maximum_fusion
  98.3 2.2 %collective-permute-start.1 = (f32[3,1]{0,1:T(1,128)S(1)}, f32[3,1]{0,1:T(1,128)S(1)}, u32[]{:S(2)}, u32[]{:S(2)}) collective-permute-start(f32[3,1]{0,1:T(1,128)S(1)} %slice.108), channel_id=1, source_target_pairs={{0,1},{1,2},{2,3},{3,4},{4,5},{5,6},{6,7},{7,8},{8,9},{9,10},{10,1... | collective-permute-start | bytes 44 | tf_op jit(solution)/shard_map/ppermute | solution.py:14
  100.6 0.7 collective-permute-done.1
  101.4 0.7 maximum_multiply_fusion
  102.1 45.5 %reduce-scatter.2.cloned.1.call-done = f32[6,128]{1,0:T(8,128)} async-done(((f32[6,2048]{1,0:T(8,128)}), f32[6,128]{1,0:T(8,128)}) %reduce-scatter.2.cloned.1.call-update) | async-done | bytes 3088 | tf_op jit(solution)/shard_map/reduce_scatter | solution.py:94
  (33 shorter events, 0.7 us)
Async XLA Ops:
  7.2 140.4 %reduce-scatter.2.cloned.1.call-start = ((), (), s32[]{:S(2)}) async-start(), calls=%async_computation.1 | async-start | bytes 69632 | tf_op jit(solution)/shard_map/reduce_scatter | solution.py:94
  7.2 64.1 %collective-permute-start = (f32[3,1]{1,0:T(4,128)}, f32[3,1]{1,0:T(4,128)S(1)}, u32[]{:S(2)}, u32[]{:S(2)}) collective-permute-start(f32[3,1]{1,0:T(4,128)} %bitcast.141), channel_id=1, source_target_pairs={{1,0},{2,1},{3,2},{4,3},{5,4},{6,5},{7,6},{8,7},{9,8},{10,9},{11,1... | collective-permute-start | bytes 44 | tf_op jit(solution)/shard_map/ppermute | solution.py:14
  74.5 0.7 copy-start.2
  74.5 0.7 copy-start.3
  89.7 3.4 %copy-start = (f32[1,128,2048]{2,1,0:T(8,128)S(1)}, f32[1,128,2048]{2,1,0:T(8,128)}, u32[]{:S(2)}) copy-start(f32[1,128,2048]{2,1,0:T(8,128)} %get-tuple-element.87) | copy-start | bytes 3145732
  93.1 4.4 %copy-start.1 = (f32[3]{0:T(128)S(1)}, f32[3]{0:T(128)}, u32[]{:S(2)}) copy-start(f32[3]{0:T(128)} %constant.34.clone) | copy-start | bytes 40
  98.3 3.1 %collective-permute-start.1 = (f32[3,1]{0,1:T(1,128)S(1)}, f32[3,1]{0,1:T(1,128)S(1)}, u32[]{:S(2)}, u32[]{:S(2)}) collective-permute-start(f32[3,1]{0,1:T(1,128)S(1)} %slice.108), channel_id=1, source_target_pairs={{0,1},{1,2},{2,3},{3,4},{4,5},{5,6},{6,7},{7,8},{8,9},{9,10},{10,1... | collective-permute-start | bytes 44 | tf_op jit(solution)/shard_map/ppermute | solution.py:14
Sparse Core Ops, SparseCore 0:
  98.4 49.1 reduce-scatter.1
where the time goes:
time: 155 us; the launch traced here: 154 us
  blocking collectives  60.7 us (39%)
  waiting for transfers between devices  46.3 us (30%)
  other arithmetic  25.1 us (16%)
  between operations  14.3 us (9%)
  starting transfers between devices  3.57 us (2%)
  local copies, waits for them, and re-layouts  2.68 us (2%)
  matrix products  1.85 us (1%)
    reduce_scatter x1, waiting for transfers between devices, on_device(): lax.psum_scatter(receiver_buffer, 'src', scatter_dimension=1, tiled=True)  45.5 us
    all_gather x1, blocking collectives, on_device(): shard_points = lax.all_gather(points, 'src', axis=1, tiled=True)  23.8 us
    all_gather x1, blocking collectives, on_device(): shard_left = lax.all_gather(left_modes, 'src', axis=1, tiled=True)  19.2 us
    all_gather x1, blocking collectives, on_device(): shard_normals = lax.all_gather(rcv_normals, 'src', axis=1, tiled=True)  17.7 us
    broadcast_in_dim x2, other arithmetic, tile_energy(): cross_z = rel_first[0] * rel_second[1] - rel_first[1] * rel_second[0]  6.79 us
    ppermute x2, starting transfers between devices, shifted(): lax.ppermute(value, axis, [(source, source + steps) for source in range(l...  3.54 us
    reduce_sum x1, other arithmetic, tile_energy(): rel_first = points[:, None, :] - first_end[:, :, None]  3.41 us
  transfers between devices with their start and end apart: 3, of which 2 were waited for; matrix products, arithmetic and copies ran while one was open for 2% of the time, Pallas kernels for 0%

commit v1 on v0

--- a/solution.py
+++ b/solution.py
@@ -1,3 +1,4 @@
+import functools
 import math
 import jax
 import jax.numpy as jnp
@@ -6,6 +7,25 @@
 
 core_term = 0.05
 inverse_four_pi = 0.25 / math.pi
+
+
+def _wait_tasks(sheet, device_axis):
+    n = lax.axis_size(device_axis)
+    by_place = tuple(((ii, (ii + 1) % n) for ii in range(n)))
+
+    def scan_the_unit(a_now):
+        if len(a_now) == n:
+            return a_now
+        fresh = lax.ppermute(a_now[0], device_axis, by_place)
+        return scan_the_unit([fresh, *a_now])
+
+    field_out = scan_the_unit([sheet])
+    local_out = jnp.concatenate(field_out, 1)
+    seen_now = lax.axis_index(device_axis)
+    return jnp.roll(local_out, (seen_now + 1) * sheet.shape[1], 1)
+
+
+_raise_counts = functools.partial(_wait_tasks, device_axis="src")
 
 
 def shifted(value, axis, steps):
@@ -71,7 +91,7 @@
         jnp.zeros((6, receiver_count), jnp.float32),
     )
     shard_points = lax.all_gather(points, "src", axis=1, tiled=True)
-    shard_normals = lax.all_gather(rcv_normals, "src", axis=1, tiled=True)
+    shard_normals = _raise_counts(rcv_normals)
     shard_left = lax.all_gather(left_modes, "src", axis=1, tiled=True)
     row_count = shard_points.shape[1]
     width_rows = math.gcd(row_count, 2048)

time: 155 us -> 200 us (1.29)
  waiting for transfers between devices: 46.3 us -> 115 us
  blocking collectives: 60.7 us -> 36.9 us
    ppermute x0 -> x15, waiting for transfers between devices: none -> 67.3 us  [scan_the_unit(): fresh = lax.ppermute(a_now[0], device_axis, by_place)]
    all_gather x1 -> x0, blocking collectives: 17.7 us -> none  [on_device(): shard_normals = lax.all_gather(rcv_normals, 'src', axis=1, tiled=True)]
    all_gather x1, blocking collectives: 23.8 us -> 18.5 us  [on_device(): shard_points = lax.all_gather(points, 'src', axis=1, tiled=True)]
  transfers between devices with their start and end apart: 3 -> 18, of which waited for: 2 -> 15; matrix products, arithmetic and copies ran while one was open for 2% -> 3% of each run, Pallas kernels for 0% -> 0%
where the time goes in v1:
time: 200 us
  waiting for transfers between devices  115 us (58%)
  blocking collectives  36.9 us (18%)
  other arithmetic  25 us (12%)
  between operations  14.4 us (7%)
  starting transfers between devices  3.65 us (2%)
  local copies, waits for them, and re-layouts  3.04 us (2%)
    ppermute x15, waiting for transfers between devices, scan_the_unit(): fresh = lax.ppermute(a_now[0], device_axis, by_place)  67.3 us
    reduce_scatter x1, waiting for transfers between devices, on_device(): lax.psum_scatter(receiver_buffer, 'src', scatter_dimension=1, tiled=True)  46.9 us
    all_gather x1, blocking collectives, on_device(): shard_points = lax.all_gather(points, 'src', axis=1, tiled=True)  18.5 us
    all_gather x1, blocking collectives, on_device(): shard_left = lax.all_gather(left_modes, 'src', axis=1, tiled=True)  18.4 us
    broadcast_in_dim x2, other arithmetic, tile_energy(): cross_z = rel_first[0] * rel_second[1] - rel_first[1] * rel_second[0]  6.8 us
  transfers between devices with their start and end apart: 18, of which 15 were waited for; matrix products, arithmetic and copies ran while one was open for 3% of the time, Pallas kernels for 0%

profile of v1, /device:TPU:0, one launch (start us, length us, event | category | flops | bytes accessed | tf_op | source)
XLA Modules:
  0.0 199.9 jit_solution(11627072109845137642)
XLA Ops:
  7.7 1.3 collective-permute-start
  9.0 5.2 %collective-permute-done.1 = f32[3,128]{1,0:T(4,128)S(1)} collective-permute-done((f32[3,128]{1,0:T(4,128)}, f32[3,128]{1,0:T(4,128)S(1)}, u32[]{:S(2)}, u32[]{:S(2)}) %collective-permute-start.1) | collective-permute-done | bytes 1568 | tf_op jit(solution)/shard_map/ppermute | solution.py:19
  14.2 0.7 multiply_add_fusion.1
  14.9 5.0 %collective-permute-done.2 = f32[3,128]{1,0:T(4,128)S(1)} collective-permute-done((f32[3,128]{1,0:T(4,128)S(1)}, f32[3,128]{1,0:T(4,128)S(1)}, u32[]{:S(2)}, u32[]{:S(2)}) %collective-permute-start.2) | collective-permute-done | bytes 1568 | tf_op jit(solution)/shard_map/ppermute | solution.py:19
  20.6 5.0 %collective-permute-done.3 = f32[3,128]{1,0:T(4,128)S(1)} collective-permute-done((f32[3,128]{1,0:T(4,128)S(1)}, f32[3,128]{1,0:T(4,128)S(1)}, u32[]{:S(2)}, u32[]{:S(2)}) %collective-permute-start.3) | collective-permute-done | bytes 1568 | tf_op jit(solution)/shard_map/ppermute | solution.py:19
  25.6 0.7 slice.81
  26.3 5.0 %collective-permute-done.4 = f32[3,128]{1,0:T(4,128)S(1)} collective-permute-done((f32[3,128]{1,0:T(4,128)S(1)}, f32[3,128]{1,0:T(4,128)S(1)}, u32[]{:S(2)}, u32[]{:S(2)}) %collective-permute-start.4) | collective-permute-done | bytes 1568 | tf_op jit(solution)/shard_map/ppermute | solution.py:19
  31.3 5.7 %collective-permute-done.5 = f32[3,128]{1,0:T(4,128)S(1)} collective-permute-done((f32[3,128]{1,0:T(4,128)S(1)}, f32[3,128]{1,0:T(4,128)S(1)}, u32[]{:S(2)}, u32[]{:S(2)}) %collective-permute-start.5) | collective-permute-done | bytes 1568 | tf_op jit(solution)/shard_map/ppermute | solution.py:19
  37.0 18.4 %all_gather.7 = f32[8,2048]{1,0:T(8,128)S(1)} all-gather(f32[8,128]{1,0:T(8,128)} %param.10), channel_id=1, replica_groups=mesh['group'=2,'src'=16] {'src'}, dimensions={1}, use_global_device_ids=true | all-gather | bytes 69632 | tf_op jit(solution)/shard_map/all_gather | solution.py:95
  55.6 18.5 %all_gather.6 = f32[3,2048]{1,0:T(4,128)S(1)} all-gather(f32[3,128]{1,0:T(4,128)S(1)} %pad_maximum_fusion.3), channel_id=1, replica_groups=mesh['group'=2,'src'=16] {'src'}, dimensions={1}, use_global_device_ids=true | all-gather | bytes 26112 | tf_op jit(solution)/shard_map/all_gather | solution.py:93
  74.5 0.8 pad_maximum_fusion.1
  75.2 4.6 %collective-permute-done.8 = f32[3,128]{1,0:T(4,128)S(1)} collective-permute-done((f32[3,128]{1,0:T(4,128)S(1)}, f32[3,128]{1,0:T(4,128)S(1)}, u32[]{:S(2)}, u32[]{:S(2)}) %collective-permute-start.8) | collective-permute-done | bytes 1568 | tf_op jit(solution)/shard_map/ppermute | solution.py:19
  79.8 5.7 %collective-permute-done.9 = f32[3,128]{1,0:T(4,128)S(1)} collective-permute-done((f32[3,128]{1,0:T(4,128)S(1)}, f32[3,128]{1,0:T(4,128)S(1)}, u32[]{:S(2)}, u32[]{:S(2)}) %collective-permute-start.9) | collective-permute-done | bytes 1568 | tf_op jit(solution)/shard_map/ppermute | solution.py:19
  87.1 4.1 %collective-permute-done.10 = f32[3,128]{1,0:T(4,128)S(1)} collective-permute-done((f32[3,128]{1,0:T(4,128)S(1)}, f32[3,128]{1,0:T(4,128)S(1)}, u32[]{:S(2)}, u32[]{:S(2)}) %collective-permute-start.10) | collective-permute-done | bytes 1568 | tf_op jit(solution)/shard_map/ppermute | solution.py:19
  91.2 0.8 fusion.15
  92.1 4.9 %collective-permute-done.11 = f32[3,128]{1,0:T(4,128)S(1)} collective-permute-done((f32[3,128]{1,0:T(4,128)S(1)}, f32[3,128]{1,0:T(4,128)S(1)}, u32[]{:S(2)}, u32[]{:S(2)}) %collective-permute-start.11) | collective-permute-done | bytes 1568 | tf_op jit(solution)/shard_map/ppermute | solution.py:19
  97.3 5.3 %collective-permute-done.12 = f32[3,128]{1,0:T(4,128)S(1)} collective-permute-done((f32[3,128]{1,0:T(4,128)S(1)}, f32[3,128]{1,0:T(4,128)S(1)}, u32[]{:S(2)}, u32[]{:S(2)}) %collective-permute-start.12) | collective-permute-done | bytes 1568 | tf_op jit(solution)/shard_map/ppermute | solution.py:19
  103.0 5.4 %collective-permute-done.13 = f32[3,128]{1,0:T(4,128)S(1)} collective-permute-done((f32[3,128]{1,0:T(4,128)S(1)}, f32[3,128]{1,0:T(4,128)S(1)}, u32[]{:S(2)}, u32[]{:S(2)}) %collective-permute-start.13) | collective-permute-done | bytes 1568 | tf_op jit(solution)/shard_map/ppermute | solution.py:19
  108.4 5.7 %collective-permute-done.14 = f32[3,128]{1,0:T(4,128)S(1)} collective-permute-done((f32[3,128]{1,0:T(4,128)S(1)}, f32[3,128]{1,0:T(4,128)S(1)}, u32[]{:S(2)}, u32[]{:S(2)}) %collective-permute-start.14) | collective-permute-done | bytes 1568 | tf_op jit(solution)/shard_map/ppermute | solution.py:19
  114.1 5.7 %collective-permute-done.15 = f32[3,128]{1,0:T(4,128)S(1)} collective-permute-done((f32[3,128]{1,0:T(4,128)S(1)}, f32[3,128]{1,0:T(4,128)S(1)}, u32[]{:S(2)}, u32[]{:S(2)}) %collective-permute-start.15) | collective-permute-done | bytes 1568 | tf_op jit(solution)/shard_map/ppermute | solution.py:19
  120.3 1.8 divide_multiply_fusion.1
  122.2 2.5 %multiply_reduce_fusion = (f32[3,128]{1,0:T(4,128)S(1)}, f32[128,2048]{1,0:T(8,128)S(1)}, f32[128,2048]{1,0:T(8,128)S(1)}, f32[128,2048]{1,0:T(8,128)S(1)}) fusion(f32[128,2048]{1,0:T(8,128)S(1)} %get-tuple-element.62, f32[128,2048]{1,0:T(8,128)S(1)} %get-tuple-element.92, f32[3,128]{1,0:T(4,128)S(1)} %bitcast.127, f32[128,2048]{1,0:T(8,128)S(1)} %get-tuple-element.94, ...), kind=kLoop, calls=%fused_computation.36 | loop fusion | flops 12582528 | bytes 8419328 | tf_op jit(solution)/shard_map/while/body/eval_jaxpr/transpose(jvp())/reduce_sum | solution.py:55
  125.6 2.0 %multiply_bitcast_fusion.5 = (f32[1,128,2048]{2,1,0:T(8,128)}, f32[128,2048]{1,0:T(8,128)}, f32[128,2048]{1,0:T(8,128)S(1)}) fusion(f32[3,128,2048]{2,1,0:T(8,128)S(1)} %get-tuple-element.98, f32[128,2048]{1,0:T(8,128)S(1)} %get-tuple-element.67, f32[128,2048]{1,0:T(8,128)S(1)} %get-tuple-element.54, f32[2048]{0:T(1024)S(1)} %broadcast_multiply_fusion.2, ...), kind=kLoop, calls=%fused_computation.57 | loop fusion | flops 2359296 | bytes 9445376 | tf_op jit(solution)/shard_map/while/body/eval_jaxpr/transpose(jvp())/broadcast_in_dim | solution.py:51
  127.6 2.3 %multiply_bitcast_fusion.3 = (f32[1,128,2048]{2,1,0:T(8,128)S(1)}, f32[128,2048]{1,0:T(8,128)}, f32[1,128,2048]{2,1,0:T(8,128)S(1)}, f32[128,2048]{1,0:T(8,128)}...) fusion(f32[3,128,2048]{2,1,0:T(8,128)S(1)} %get-tuple-element.98, f32[128,2048]{1,0:T(8,128)S(1)} %get-tuple-element.66, ...), kind=kLoop, calls=%fused_computation.55 | loop fusion | flops 5236736 | bytes 11575296 | tf_op jit(solution)/shard_map/while/body/eval_jaxpr/transpose(jvp())/broadcast_in_dim | solution.py:50
  129.8 4.8 %multiply_bitcast_fusion.11 = (f32[1,128,2048]{2,1,0:T(8,128)S(1)}, f32[1,128,2048]{2,1,0:T(8,128)S(1)}, f32[1,128,2048]{2,1,0:T(8,128)S(1)}, f32[1,128,2048]{2,...) fusion(f32[128,2048]{1,0:T(8,128)} %get-tuple-element.56, ...), kind=kLoop, calls=%fused_computation.65 | loop fusion | flops 3145728 | bytes 18874368 | tf_op jit(solution)/shard_map/while/body/eval_jaxpr/transpose(jvp())/broadcast_in_dim | solution.py:51
  134.6 3.4 %fusion.27 = (f32[3,128]{1,0:T(4,128)S(1)}, f32[3,2048]{1,0:T(4,128)S(1)}) fusion(f32[1,128,2048]{2,1,0:T(8,128)} %get-tuple-element.88, f32[1,128,2048]{2,1,0:T(8,128)S(1)} %get-tuple-element.70, f32[1,128,2048]{2,1,0:T(8,128)} %get-tuple-element.89, f32[1,128,2048]{2,1,0:T(8,128)S(1)} %get-tuple-element.58, f32[1,128,2048]{2,1,0:T(8,128)} %get-tuple-element.90, ...), kind=kLoop, calls=%fused_computation.144 | loop fusion | flops 11003520 | bytes 9490944 | tf_op jit(solution)/shard_map/while/body/eval_jaxpr/transpose(jvp())/reduce_sum | solution.py:46
  138.1 1.9 fusion.26
  140.2 1.0 scatter_custom_fusion
  141.2 1.2 scatter_fusion
  143.2 1.3 collective-permute-start.16
  144.6 0.7 collective-permute-done.16
  146.1 46.9 %reduce-scatter.2.cloned.1.call-done = f32[6,128]{1,0:T(8,128)} async-done(((f32[6,2048]{1,0:T(8,128)}), f32[6,128]{1,0:T(8,128)}) %reduce-scatter.2.cloned.1.call-update) | async-done | bytes 3088 | tf_op jit(solution)/shard_map/reduce_scatter | solution.py:114
  (96 shorter events, 7.2 us)
Async XLA Ops:
  7.2 185.8 %reduce-scatter.2.cloned.1.call-start = ((), (), s32[]{:S(2)}) async-start(), calls=%async_computation.1 | async-start | bytes 69632 | tf_op jit(solution)/shard_map/reduce_scatter | solution.py:114
  7.2 7.0 %collective-permute-start.1 = (f32[3,128]{1,0:T(4,128)}, f32[3,128]{1,0:T(4,128)S(1)}, u32[]{:S(2)}, u32[]{:S(2)}) collective-permute-start(f32[3,128]{1,0:T(4,128)} %param.9), channel_id=1, source_target_pairs={{0,1},{1,2},{2,3},{3,4},{4,5},{5,6},{6,7},{7,8},{8,9},{9,10},{10,1... | collective-permute-start | bytes 4616 | tf_op jit(solution)/shard_map/ppermute | solution.py:19
  7.7 66.7 %collective-permute-start = (f32[3,1]{1,0:T(4,128)}, f32[3,1]{1,0:T(4,128)S(1)}, u32[]{:S(2)}, u32[]{:S(2)}) collective-permute-start(f32[3,1]{1,0:T(4,128)} %bitcast.141), channel_id=1, source_target_pairs={{1,0},{2,1},{3,2},{4,3},{5,4},{6,5},{7,6},{8,7},{9,8},{10,9},{11,1... | collective-permute-start | bytes 44 | tf_op jit(solution)/shard_map/ppermute | solution.py:34
  14.2 5.7 %collective-permute-start.2 = (f32[3,128]{1,0:T(4,128)S(1)}, f32[3,128]{1,0:T(4,128)S(1)}, u32[]{:S(2)}, u32[]{:S(2)}) collective-permute-start(f32[3,128]{1,0:T(4,128)S(1)} %collective-permute-done.1), channel_id=1, source_target_pairs={{0,1},{1,2},{2,3},{3,4},{4,5},{5,6},{6,7},{7,8},{8,9},{9,10},{10,1... | collective-permute-start | bytes 4616 | tf_op jit(solution)/shard_map/ppermute | solution.py:19
  19.9 5.7 %collective-permute-start.3 = (f32[3,128]{1,0:T(4,128)S(1)}, f32[3,128]{1,0:T(4,128)S(1)}, u32[]{:S(2)}, u32[]{:S(2)}) collective-permute-start(f32[3,128]{1,0:T(4,128)S(1)} %collective-permute-done.2), channel_id=1, source_target_pairs={{0,1},{1,2},{2,3},{3,4},{4,5},{5,6},{6,7},{7,8},{8,9},{9,10},{10,1... | collective-permute-start | bytes 4616 | tf_op jit(solution)/shard_map/ppermute | solution.py:19
  25.6 5.7 %collective-permute-start.4 = (f32[3,128]{1,0:T(4,128)S(1)}, f32[3,128]{1,0:T(4,128)S(1)}, u32[]{:S(2)}, u32[]{:S(2)}) collective-permute-start(f32[3,128]{1,0:T(4,128)S(1)} %collective-permute-done.3), channel_id=1, source_target_pairs={{0,1},{1,2},{2,3},{3,4},{4,5},{5,6},{6,7},{7,8},{8,9},{9,10},{10,1... | collective-permute-start | bytes 4616 | tf_op jit(solution)/shard_map/ppermute | solution.py:19
  31.3 5.7 %collective-permute-start.5 = (f32[3,128]{1,0:T(4,128)S(1)}, f32[3,128]{1,0:T(4,128)S(1)}, u32[]{:S(2)}, u32[]{:S(2)}) collective-permute-start(f32[3,128]{1,0:T(4,128)S(1)} %collective-permute-done.4), channel_id=1, source_target_pairs={{0,1},{1,2},{2,3},{3,4},{4,5},{5,6},{6,7},{7,8},{8,9},{9,10},{10,1... | collective-permute-start | bytes 4616 | tf_op jit(solution)/shard_map/ppermute | solution.py:19
  37.0 18.4 %collective-permute-start.6 = (f32[3,128]{1,0:T(4,128)S(1)}, f32[3,128]{1,0:T(4,128)S(1)}, u32[]{:S(2)}, u32[]{:S(2)}) collective-permute-start(f32[3,128]{1,0:T(4,128)S(1)} %collective-permute-done.5), channel_id=1, source_target_pairs={{0,1},{1,2},{2,3},{3,4},{4,5},{5,6},{6,7},{7,8},{8,9},{9,10},{10,1... | collective-permute-start | bytes 4616 | tf_op jit(solution)/shard_map/ppermute | solution.py:19
  55.4 18.7 %collective-permute-start.7 = (f32[3,128]{1,0:T(4,128)S(1)}, f32[3,128]{1,0:T(4,128)S(1)}, u32[]{:S(2)}, u32[]{:S(2)}) collective-permute-start(f32[3,128]{1,0:T(4,128)S(1)} %collective-permute-done.6), channel_id=1, source_target_pairs={{0,1},{1,2},{2,3},{3,4},{4,5},{5,6},{6,7},{7,8},{8,9},{9,10},{10,1... | collective-permute-start | bytes 4616 | tf_op jit(solution)/shard_map/ppermute | solution.py:19
  74.1 5.7 %collective-permute-start.8 = (f32[3,128]{1,0:T(4,128)S(1)}, f32[3,128]{1,0:T(4,128)S(1)}, u32[]{:S(2)}, u32[]{:S(2)}) collective-permute-start(f32[3,128]{1,0:T(4,128)S(1)} %collective-permute-done.7), channel_id=1, source_target_pairs={{0,1},{1,2},{2,3},{3,4},{4,5},{5,6},{6,7},{7,8},{8,9},{9,10},{10,1... | collective-permute-start | bytes 4616 | tf_op jit(solution)/shard_map/ppermute | solution.py:19
  79.8 5.7 %collective-permute-start.9 = (f32[3,128]{1,0:T(4,128)S(1)}, f32[3,128]{1,0:T(4,128)S(1)}, u32[]{:S(2)}, u32[]{:S(2)}) collective-permute-start(f32[3,128]{1,0:T(4,128)S(1)} %collective-permute-done.8), channel_id=1, source_target_pairs={{0,1},{1,2},{2,3},{3,4},{4,5},{5,6},{6,7},{7,8},{8,9},{9,10},{10,1... | collective-permute-start | bytes 4616 | tf_op jit(solution)/shard_map/ppermute | solution.py:19
  85.5 5.7 %collective-permute-start.10 = (f32[3,128]{1,0:T(4,128)S(1)}, f32[3,128]{1,0:T(4,128)S(1)}, u32[]{:S(2)}, u32[]{:S(2)}) collective-permute-start(f32[3,128]{1,0:T(4,128)S(1)} %collective-permute-done.9), channel_id=1, source_target_pairs={{0,1},{1,2},{2,3},{3,4},{4,5},{5,6},{6,7},{7,8},{8,9},{9,10},{10,1... | collective-permute-start | bytes 4616 | tf_op jit(solution)/shard_map/ppermute | solution.py:19
  91.2 5.7 %collective-permute-start.11 = (f32[3,128]{1,0:T(4,128)S(1)}, f32[3,128]{1,0:T(4,128)S(1)}, u32[]{:S(2)}, u32[]{:S(2)}) collective-permute-start(f32[3,128]{1,0:T(4,128)S(1)} %collective-permute-done.10), channel_id=1, source_target_pairs={{0,1},{1,2},{2,3},{3,4},{4,5},{5,6},{6,7},{7,8},{8,9},{9,10},{10,1... | collective-permute-start | bytes 4616 | tf_op jit(solution)/shard_map/ppermute | solution.py:19
  96.9 5.7 %collective-permute-start.12 = (f32[3,128]{1,0:T(4,128)S(1)}, f32[3,128]{1,0:T(4,128)S(1)}, u32[]{:S(2)}, u32[]{:S(2)}) collective-permute-start(f32[3,128]{1,0:T(4,128)S(1)} %collective-permute-done.11), channel_id=1, source_target_pairs={{0,1},{1,2},{2,3},{3,4},{4,5},{5,6},{6,7},{7,8},{8,9},{9,10},{10,1... | collective-permute-start | bytes 4616 | tf_op jit(solution)/shard_map/ppermute | solution.py:19
  97.0 23.0 %copy-start.1 = (f32[3,128]{1,0:T(4,128)S(1)}, f32[3,128]{1,0:T(4,128)}, u32[]{:S(2)}) copy-start(f32[3,128]{1,0:T(4,128)} %param.9) | copy-start | bytes 4612
  97.0 23.3 %copy-start.3 = (f32[8,128]{1,0:T(8,128)S(1)}, f32[8,128]{1,0:T(8,128)}, u32[]{:S(2)}) copy-start(f32[8,128]{1,0:T(8,128)} %param.13) | copy-start | bytes 12292
  97.0 23.3 %copy-start.4 = (f32[8]{0:T(128)S(1)}, f32[8]{0:T(128)}, u32[]{:S(2)}) copy-start(f32[8]{0:T(128)} %param.14) | copy-start | bytes 100
  102.7 5.7 %collective-permute-start.13 = (f32[3,128]{1,0:T(4,128)S(1)}, f32[3,128]{1,0:T(4,128)S(1)}, u32[]{:S(2)}, u32[]{:S(2)}) collective-permute-start(f32[3,128]{1,0:T(4,128)S(1)} %collective-permute-done.12), channel_id=1, source_target_pairs={{0,1},{1,2},{2,3},{3,4},{4,5},{5,6},{6,7},{7,8},{8,9},{9,10},{10,1... | collective-permute-start | bytes 4616 | tf_op jit(solution)/shard_map/ppermute | solution.py:19
  108.4 5.7 %collective-permute-start.14 = (f32[3,128]{1,0:T(4,128)S(1)}, f32[3,128]{1,0:T(4,128)S(1)}, u32[]{:S(2)}, u32[]{:S(2)}) collective-permute-start(f32[3,128]{1,0:T(4,128)S(1)} %collective-permute-done.13), channel_id=1, source_target_pairs={{0,1},{1,2},{2,3},{3,4},{4,5},{5,6},{6,7},{7,8},{8,9},{9,10},{10,1... | collective-permute-start | bytes 4616 | tf_op jit(solution)/shard_map/ppermute | solution.py:19
  114.1 5.7 %collective-permute-start.15 = (f32[3,128]{1,0:T(4,128)S(1)}, f32[3,128]{1,0:T(4,128)S(1)}, u32[]{:S(2)}, u32[]{:S(2)}) collective-permute-start(f32[3,128]{1,0:T(4,128)S(1)} %collective-permute-done.14), channel_id=1, source_target_pairs={{0,1},{1,2},{2,3},{3,4},{4,5},{5,6},{6,7},{7,8},{8,9},{9,10},{10,1... | collective-permute-start | bytes 4616 | tf_op jit(solution)/shard_map/ppermute | solution.py:19
  134.6 3.4 %copy-start = (f32[1,128,2048]{2,1,0:T(8,128)S(1)}, f32[1,128,2048]{2,1,0:T(8,128)}, u32[]{:S(2)}) copy-start(f32[1,128,2048]{2,1,0:T(8,128)} %get-tuple-element.87) | copy-start | bytes 3145732
  138.0 4.4 %copy-start.2 = (f32[3]{0:T(128)S(1)}, f32[3]{0:T(128)}, u32[]{:S(2)}) copy-start(f32[3]{0:T(128)} %constant.73.clone) | copy-start | bytes 40
  143.2 2.1 %collective-permute-start.16 = (f32[3,1]{0,1:T(1,128)S(1)}, f32[3,1]{0,1:T(1,128)S(1)}, u32[]{:S(2)}, u32[]{:S(2)}) collective-permute-start(f32[3,1]{0,1:T(1,128)S(1)} %slice.105), channel_id=1, source_target_pairs={{0,1},{1,2},{2,3},{3,4},{4,5},{5,6},{6,7},{7,8},{8,9},{9,10},{10,1... | collective-permute-start | bytes 44 | tf_op jit(solution)/shard_map/ppermute | solution.py:34
Sparse Core Ops, SparseCore 0:
  143.3 49.6 reduce-scatter.1
